TPU v7x, 32 devices: a whole 2x2x4 slice. The times are simulated.
32 devices in a mesh: groups: 2 (over y), rows: 4 (over z), blocks: 2 (over x), cols: 2 (over core).
Axes of the slice: x: 2, y: 2, z: 4, core: 2. Of those that a mesh axis runs over, the one named last changes fastest.
Arguments:
- inputs: bfloat16 [4096, 1024], P(('groups', 'rows')), parts along dimension 0, may hold values from -6 to 6
- projection: bfloat16 [1024, 8192], P(None, ('groups', 'blocks', 'cols')), parts along dimension 1, may hold values from -0.1875 to 0.1875
- phases: bfloat16 [8192], P(('groups', 'blocks', 'cols')), parts along dimension 0, may hold values from -3.140625 to 3.140625
- inverse_blocks: float32 [4, 2048, 2048], P(('groups', 'blocks'), 'rows'), parts along dimension 0, as said below
- labels: int32 [4096], P(('groups', 'rows')), parts along dimension 0, may hold values from 0 to 999
- predictions: float32 [4096, 1000], P(('groups', 'rows'), 'cols'), parts along dimension 0, may hold values from -4 to 4
- coefficients: float32 [8192, 1000], P(('groups', 'blocks', 'rows'), 'cols'), parts along dimension 0, may hold values from -3 to 3
Outputs:
- new_coefficients: float32 [8192, 1000], P(('groups', 'blocks', 'rows'), 'cols'), parts along dimension 0
- new_predictions: float32 [4096, 1000], P(('groups', 'rows'), 'cols'), parts along dimension 0
There are 2 independent parts, one for each index of `groups`. A program takes and returns all parts, laid end to end along the dimension named above; each array names one. Nothing has to cross between parts.
Inputs may be any that keep to these rules, and one draw needn't show every extreme that they name: `inverse_blocks`: one dense preconditioner for each feature block.
All inputs are finite; a program needn't handle non-finite values.
Results may differ from a plain program's by a relative error of at most 0.0029.
Values may be sent and summed in bfloat16 or wider, within the bound.
No kernel may reach another device: no remote copies, remote signals or barrier semaphores. Data moves between devices by JAX's collectives and lax.ppermute only.
A program may use at most 64 MiB of HBM per device.

v0:
```python
import jax
import jax.numpy as jnp
from jax import lax
from jax.sharding import PartitionSpec as P

DAMPING = 0.5


def cosine_features(inputs, projection, phases):
    angles = (
        jnp.dot(inputs, projection, preferred_element_type=jnp.float32)
        + phases.astype(jnp.float32)[None, :]
    )
    return jnp.cos(angles).astype(jnp.bfloat16)


def shards(inputs, projection, phases, inverse_blocks, labels, predictions, coefficients):
    out_width = predictions.shape[1]
    classes = lax.axis_index("cols") * out_width + jnp.arange(out_width, dtype=jnp.int32)
    onehot = (labels[:, None] == classes[None, :]).astype(jnp.float32)
    residual = (onehot - predictions).astype(jnp.bfloat16)
    half_features = cosine_features(inputs, projection, phases)
    features_full = lax.all_gather(half_features, "cols", axis=1, tiled=True)
    local_inverse = inverse_blocks[0]
    column_slice = features_full
    own_gradient = lax.psum_scatter(
        lax.dot_general(
            column_slice, residual, (((0,), (0,)), ((), ())), preferred_element_type=jnp.float32
        ),
        "rows",
        scatter_dimension=0,
        tiled=True,
    )
    gradient = lax.all_gather(own_gradient, "rows", axis=0, tiled=True)
    solved = jnp.dot(local_inverse, gradient, precision=lax.Precision.HIGHEST)
    step_update = DAMPING * solved
    new_coefficients = coefficients + step_update
    column_slice = features_full
    contribution = jnp.dot(
        column_slice,
        lax.all_gather(step_update.astype(jnp.bfloat16), "rows", axis=0, tiled=True),
        preferred_element_type=jnp.float32,
    )
    summed = lax.psum(contribution, "blocks")
    return (new_coefficients, predictions + summed)


def solution(mesh):
    return jax.shard_map(
        shards,
        mesh=mesh,
        in_specs=(
            P(("groups", "rows"), None),
            P(None, ("groups", "blocks", "cols")),
            P(("groups", "blocks", "cols")),
            P(("groups", "blocks"), "rows", None),
            P(("groups", "rows")),
            P(("groups", "rows"), "cols"),
            P(("groups", "blocks", "rows"), "cols"),
        ),
        out_specs=(P(("groups", "blocks", "rows"), "cols"), P(("groups", "rows"), "cols")),
        check_vma=False,
    )
```

profile of v0, /device:TPU:0, one launch (start us, length us, event | category | flops | bytes accessed | tf_op | source)
XLA Modules:
  0.0 311.2 jit_solution(1773116370345842166)
XLA Ops:
  7.2 0.0 copy-start
  7.2 0.0 all-gather.4.cloned.1.call-start
  7.2 0.8 convert_element_type.15
  8.0 0.7 copy-done
  8.8 0.0 copy-start.1
  8.8 0.0 copy-start.2
  8.8 9.8 %cosine_convert_fusion = bf16[512,1024]{1,0:T(8,128)(2,1)} fusion(bf16[512,1024]{1,0:T(8,128)(2,1)} %param.7, bf16[1024,1024]{1,0:T(8,128)(2,1)S(1)} %copy-done, f32[1024]{0:T(1024)S(1)} %convert_element_type.15), kind=kOutput, calls=%fused_computation.2 | convolution fusion | flops 1074790400 | bytes 4198400 | tf_op jit(solution)/shard_map/dot_general | solution.py:11
  18.6 0.0 all-gather.4.cloned.1.call-update
  18.6 0.0 reduce-scatter.2.cloned.1.call-start
  18.7 13.4 %all-gather.4.cloned.1.call-done = bf16[512,2048]{1,0:T(8,128)(2,1)} async-done(((bf16[512,1024]{1,0:T(8,128)(2,1)}), bf16[512,2048]{1,0:T(8,128)(2,1)}) %all-gather.4.cloned.1.call-update) | async-done | bytes 2097168 | tf_op jit(solution)/shard_map/all_gather | solution.py:23
  32.1 0.0 copy-done.1
  32.1 0.0 copy-done.2
  32.1 5.0 %fusion.8 = f32[2048,500]{1,0:T(8,128)} fusion(bf16[512,2048]{1,0:T(8,128)(2,1)} %all-gather.4.cloned.1.call-done, f32[512,500]{0,1:T(8,128)S(1)} %copy-done.1, s32[512]{0:T(512)S(1)} %copy-done.2, s32[500]{0:T(512)S(1)} %iota_add_fusion), kind=kOutput, calls=%fused_computation.6 | convolution fusion | flops 1049600000 | bytes 7221200 | tf_op jit(solution)/shard_map/dot_general | solution.py:27
  37.0 0.0 reduce-scatter.2.cloned.1.call-update
  37.0 0.0 all-gather.6.cloned.1.call-start
  37.1 78.0 %reduce-scatter.2.cloned.1.call-done = f32[512,500]{1,0:T(8,128)} async-done(((f32[2048,500]{1,0:T(8,128)}), f32[512,500]{1,0:T(8,128)}) %reduce-scatter.2.cloned.1.call-update) | async-done | bytes 1024016 | tf_op jit(solution)/shard_map/reduce_scatter | solution.py:26
  115.1 0.0 all-gather.6.cloned.1.call-update
  115.2 0.2 all-gather.8.cloned.1.call-start
  115.4 82.7 %all-gather.6.cloned.1.call-done = f32[2048,500]{1,0:T(8,128)} async-done(((f32[512,500]{1,0:T(8,128)}), f32[2048,500]{1,0:T(8,128)}) %all-gather.6.cloned.1.call-update) | async-done | bytes 4096016 | tf_op jit(solution)/shard_map/all_gather | solution.py:34
  198.1 17.2 %fusion.11 = (bf16[512,500]{0,1:T(8,128)(2,1)}, f32[512,500]{0,1:T(8,128)}) fusion(f32[512,500]{0,1:T(8,128)} %param.13, f32[2048,500]{1,0:T(8,128)} %all-gather.6.cloned.1.call-done, f32[1,512,2048]{2,1,0:T(8,128)} %param.10), kind=kOutput, calls=%fused_computation.10 | convolution fusion | flops 6292224000 | bytes 10850304 | tf_op jit(solution)/shard_map/dot_general | solution.py:35
  215.3 0.0 all-gather.8.cloned.1.call-update
  215.3 0.0 all-reduce.2.cloned.1.call-start
  215.4 43.9 %all-gather.8.cloned.1.call-done = bf16[2048,500]{0,1:T(8,128)(2,1)} async-done(((bf16[512,500]{0,1:T(8,128)(2,1)}), bf16[2048,500]{0,1:T(8,128)(2,1)}) %all-gather.8.cloned.1.call-update) | async-done | bytes 2048016 | tf_op jit(solution)/shard_map/all_gather | solution.py:41
  259.3 4.4 %fusion.12 = f32[512,500]{0,1:T(8,128)} fusion(bf16[512,2048]{1,0:T(8,128)(2,1)} %all-gather.4.cloned.1.call-done, bf16[2048,500]{0,1:T(8,128)(2,1)} %all-gather.8.cloned.1.call-done), kind=kOutput, calls=%fused_computation.11 | convolution fusion | flops 1048576000 | bytes 5169152 | tf_op jit(solution)/shard_map/dot_general | solution.py:39
  263.7 0.0 all-reduce.2.cloned.1.call-update
  263.8 38.6 %all-reduce.2.cloned.1.call-done = f32[512,500]{0,1:T(8,128)} async-done(((f32[512,500]{0,1:T(8,128)}), f32[512,500]{0,1:T(8,128)}) %all-reduce.2.cloned.1.call-update) | async-done | bytes 1024016 | tf_op jit(solution)/shard_map/psum | solution.py:44
  302.3 2.4 add.33
  (1 shorter events, 0.0 us)
Async XLA Ops:
  7.2 1.6 copy-start
  7.2 24.9 %all-gather.4.cloned.1.call-start = ((), (), s32[]{:S(2)}) async-start(), calls=%async_computation.1 | async-start | bytes 3145728 | tf_op jit(solution)/shard_map/all_gather | solution.py:23
  8.8 23.3 %copy-start.1 = (f32[512,500]{0,1:T(8,128)S(1)}, f32[512,500]{0,1:T(8,128)}, u32[]{:S(2)}) copy-start(f32[512,500]{0,1:T(8,128)} %param.12) | copy-start | bytes 3072004
  8.8 23.3 %copy-start.2 = (s32[512]{0:T(512)S(1)}, s32[512]{0:T(512)}, u32[]{:S(2)}) copy-start(s32[512]{0:T(512)} %param.11) | copy-start | bytes 6148
  18.6 96.5 %reduce-scatter.2.cloned.1.call-start = ((), (), s32[]{:S(2)}) async-start(), calls=%async_computation.2 | async-start | bytes 5242880 | tf_op jit(solution)/shard_map/reduce_scatter | solution.py:26
  37.0 161.1 %all-gather.6.cloned.1.call-start = ((), (), s32[]{:S(2)}) async-start(), calls=%async_computation.3 | async-start | bytes 5242880 | tf_op jit(solution)/shard_map/all_gather | solution.py:34
  115.2 144.1 %all-gather.8.cloned.1.call-start = ((), (), s32[]{:S(2)}) async-start(), calls=%async_computation.4 | async-start | bytes 2580480 | tf_op jit(solution)/shard_map/all_gather | solution.py:41
  215.3 87.0 %all-reduce.2.cloned.1.call-start = ((), (), s32[]{:S(2)}) async-start(), calls=%async_computation.5 | async-start | bytes 2064384 | tf_op jit(solution)/shard_map/psum | solution.py:44
Sparse Core Ops, SparseCore 0:
  18.7 13.2 all-gather.3
  37.2 77.9 reduce-scatter.1
  116.8 81.2 all-gather.5
  215.4 43.8 all-gather.7
  263.9 38.3 all-reduce.1
where the time goes:
time: 311 us
  waiting for transfers between devices  257 us (83%)
  matrix products  36.4 us (12%)
  between operations  13.8 us (4%)
  other arithmetic  3.21 us (1%)
    all_gather x1, waiting for transfers between devices, shards(): gradient = lax.all_gather(own_gradient, 'rows', axis=0, tiled=True)  82.7 us
    reduce_scatter x1, waiting for transfers between devices, shards(): lax.psum_scatter(lax.dot_general(column_slice, residual, (((0,), (0,)), (...  78 us
    all_gather x1, waiting for transfers between devices, shards(): lax.all_gather(step_update.astype(jnp.bfloat16), 'rows', axis=0, tiled=True)  43.9 us
    psum x1, waiting for transfers between devices, shards(): summed = lax.psum(contribution, 'blocks')  38.6 us
    dot_general x1, matrix products, shards(): solved = jnp.dot(local_inverse, gradient, precision=lax.Precision.HIGHEST)  17.2 us
    all_gather x1, waiting for transfers between devices, shards(): features_full = lax.all_gather(half_features, 'cols', axis=1, tiled=True)  13.4 us
    dot_general x1, matrix products, cosine_features(): jnp.dot(inputs, projection, preferred_element_type=jnp.float32)  9.81 us
  transfers between devices with their start and end apart: 5, of which 5 were waited for; matrix products, arithmetic and copies ran while one was open for 0% of the time, Pallas kernels for 0%

commit v1 on v0

--- a/solution.py
+++ b/solution.py
@@ -31,7 +31,14 @@
         scatter_dimension=0,
         tiled=True,
     )
-    gradient = lax.all_gather(own_gradient, "rows", axis=0, tiled=True)
+    size = lax.axis_size("rows")
+    forward = [(i, (i + 1) % size) for i in range(size)]
+    parts = [own_gradient]
+    for stride in range(1, size):
+        parts = [lax.ppermute(parts[0], "rows", forward), *parts]
+    out = jnp.concatenate(parts, axis=0)
+    places = (lax.axis_index("rows") + 1) * parts[-1].shape[0]
+    gradient = jnp.roll(out, places, axis=0)
     solved = jnp.dot(local_inverse, gradient, precision=lax.Precision.HIGHEST)
     step_update = DAMPING * solved
     new_coefficients = coefficients + step_update

time: 311 us -> 302 us (0.971)
  matrix products: 36.4 us -> 27 us
  waiting for transfers between devices: 257 us -> 248 us
  local copies, waits for them, and re-layouts: 0.74 us -> 7.84 us
    all_gather x1 -> x0, waiting for transfers between devices: 82.7 us -> none  [shards(): gradient = lax.all_gather(own_gradient, 'rows', axis=0, tiled=True)]
    ppermute x0 -> x3, waiting for transfers between devices: none -> 75.4 us  [shards(): parts = [lax.ppermute(parts[0], 'rows', forward), *parts]]
    dot_general x1, matrix products: 17.2 us -> 7.93 us  [shards(): solved = jnp.dot(local_inverse, gradient, precision=lax.Precision.HIGHEST)]
    unnamed x6 -> x23, local copies, waits for them, and re-layouts: 0.74 us -> 7.75 us
  transfers between devices with their start and end apart: 5 -> 7, of which waited for: 5 -> 7; matrix products, arithmetic and copies ran while one was open for 0% -> 0% of each run, Pallas kernels for 0% -> 0%
where the time goes in v1:
time: 302 us
  waiting for transfers between devices  248 us (82%)
  matrix products  27 us (9%)
  between operations  13.9 us (5%)
  local copies, waits for them, and re-layouts  7.84 us (3%)
  other arithmetic  3.21 us (1%)
    reduce_scatter x1, waiting for transfers between devices, shards(): lax.psum_scatter(lax.dot_general(column_slice, residual, (((0,), (0,)), (...  77 us
    ppermute x3, waiting for transfers between devices, shards(): parts = [lax.ppermute(parts[0], 'rows', forward), *parts]  75.4 us
    all_gather x1, waiting for transfers between devices, shards(): lax.all_gather(step_update.astype(jnp.bfloat16), 'rows', axis=0, tiled=True)  43.5 us
    psum x1, waiting for transfers between devices, shards(): summed = lax.psum(contribution, 'blocks')  38.6 us
    all_gather x1, waiting for transfers between devices, shards(): features_full = lax.all_gather(half_features, 'cols', axis=1, tiled=True)  13.4 us
    dot_general x1, matrix products, cosine_features(): jnp.dot(inputs, projection, preferred_element_type=jnp.float32)  9.82 us
    dot_general x1, matrix products, shards(): solved = jnp.dot(local_inverse, gradient, precision=lax.Precision.HIGHEST)  7.93 us
    unnamed x23, local copies, waits for them, and re-layouts  7.75 us
  transfers between devices with their start and end apart: 7, of which 7 were waited for; matrix products, arithmetic and copies ran while one was open for 0% of the time, Pallas kernels for 0%

profile of v1, /device:TPU:0, one launch (start us, length us, event | category | flops | bytes accessed | tf_op | source)
XLA Modules:
  0.0 301.5 jit_solution(2785223272854950324)
XLA Ops:
  7.2 0.0 all-gather.3.cloned.1.call-start
  7.2 0.8 convert_element_type.15
  8.0 0.7 copy-done
  8.8 9.8 %cosine_convert_fusion = bf16[512,1024]{1,0:T(8,128)(2,1)} fusion(bf16[512,1024]{1,0:T(8,128)(2,1)} %param.7, bf16[1024,1024]{1,0:T(8,128)(2,1)S(1)} %copy-done, f32[1024]{0:T(1024)S(1)} %convert_element_type.15), kind=kOutput, calls=%fused_computation.3 | convolution fusion | flops 1074790400 | bytes 4198400 | tf_op jit(solution)/shard_map/dot_general | solution.py:11
  18.6 0.0 all-gather.3.cloned.1.call-update
  18.6 0.0 reduce-scatter.2.cloned.1.call-start
  18.7 13.4 %all-gather.3.cloned.1.call-done = bf16[512,2048]{1,0:T(8,128)(2,1)} async-done(((bf16[512,1024]{1,0:T(8,128)(2,1)}), bf16[512,2048]{1,0:T(8,128)(2,1)}) %all-gather.3.cloned.1.call-update) | async-done | bytes 2097168 | tf_op jit(solution)/shard_map/all_gather | solution.py:23
  32.1 4.8 %fusion.13 = f32[2048,500]{0,1:T(8,128)} fusion(bf16[512,2048]{1,0:T(8,128)(2,1)} %all-gather.3.cloned.1.call-done, f32[512,500]{0,1:T(8,128)S(1)} %copy-done.2, s32[512]{0:T(512)S(1)} %copy-done.7, s32[500]{0:T(512)S(1)} %iota_add_fusion), kind=kOutput, calls=%fused_computation.7 | convolution fusion | flops 1049600000 | bytes 7221200 | tf_op jit(solution)/shard_map/dot_general | solution.py:27
  36.9 0.0 reduce-scatter.2.cloned.1.call-update
  36.9 0.0 all-gather.5.cloned.1.call-start
  36.9 77.0 %reduce-scatter.2.cloned.1.call-done = f32[512,500]{0,1:T(8,128)} async-done(((f32[2048,500]{0,1:T(8,128)}), f32[512,500]{0,1:T(8,128)}) %reduce-scatter.2.cloned.1.call-update) | async-done | bytes 1024016 | tf_op jit(solution)/shard_map/reduce_scatter | solution.py:26
  114.0 1.4 collective-permute-start
  115.4 25.1 %collective-permute-done = f32[512,500]{0,1:T(8,128)S(1)} collective-permute-done((f32[512,500]{0,1:T(8,128)}, f32[512,500]{0,1:T(8,128)S(1)}, u32[]{:S(2)}, u32[]{:S(2)}) %collective-permute-start) | collective-permute-done | bytes 1024032 | tf_op jit(solution)/shard_map/ppermute | solution.py:38
  140.5 1.0 copy-done.4
  141.4 25.5 %collective-permute-done.1 = f32[512,500]{0,1:T(8,128)} collective-permute-done((f32[512,500]{0,1:T(8,128)S(1)}, f32[512,500]{0,1:T(8,128)}, u32[]{:S(2)}, u32[]{:S(2)}) %collective-permute-start.1) | collective-permute-done | bytes 1024032 | tf_op jit(solution)/shard_map/ppermute | solution.py:38
  167.0 24.8 %collective-permute-done.2 = f32[512,500]{0,1:T(8,128)} collective-permute-done((f32[512,500]{0,1:T(8,128)}, f32[512,500]{0,1:T(8,128)}, u32[]{:S(2)}, u32[]{:S(2)}) %collective-permute-start.2) | collective-permute-done | bytes 1024032 | tf_op jit(solution)/shard_map/ppermute | solution.py:38
  191.8 1.3 constant_dynamic-update-slice_fusion.7
  193.1 1.3 constant_dynamic-update-slice_fusion.6
  194.4 0.1 constant_dynamic-update-slice_fusion.5
  194.5 0.1 constant_dynamic-update-slice_fusion.4
  194.6 1.5 constant_dynamic-update-slice_fusion.3
  196.1 1.7 constant_dynamic-update-slice_fusion.2
  197.8 0.1 constant_dynamic-update-slice_fusion.1
  197.9 0.1 constant_dynamic-update-slice_fusion
  198.0 7.9 %fusion.17 = (bf16[512,500]{0,1:T(8,128)(2,1)}, f32[512,500]{0,1:T(8,128)}) fusion(f32[512,500]{0,1:T(8,128)S(1)} %copy-done.6, f32[1,512,2048]{2,1,0:T(8,128)S(1)} %copy-done.1, f32[4096,500]{0,1:T(8,128)S(1)} %constant_dynamic-update-slice_fusion, s32[]{:T(128)S(6)} %select_n.14), kind=kOutput, calls=%fused_computation.20 | convolution fusion | flops 6292224000 | bytes 10891268 | tf_op jit(solution)/shard_map/dot_general | solution.py:42
  206.0 0.0 all-gather.5.cloned.1.call-update
  206.0 0.0 all-reduce.2.cloned.1.call-start
  206.0 43.5 %all-gather.5.cloned.1.call-done = bf16[2048,500]{0,1:T(8,128)(2,1)} async-done(((bf16[512,500]{0,1:T(8,128)(2,1)}), bf16[2048,500]{0,1:T(8,128)(2,1)}) %all-gather.5.cloned.1.call-update) | async-done | bytes 2048016 | tf_op jit(solution)/shard_map/all_gather | solution.py:48
  249.6 4.4 %fusion.18 = f32[512,500]{0,1:T(8,128)} fusion(bf16[512,2048]{1,0:T(8,128)(2,1)} %all-gather.3.cloned.1.call-done, bf16[2048,500]{0,1:T(8,128)(2,1)} %all-gather.5.cloned.1.call-done), kind=kOutput, calls=%fused_computation.21 | convolution fusion | flops 1048576000 | bytes 5169152 | tf_op jit(solution)/shard_map/dot_general | solution.py:46
  254.0 0.0 all-reduce.2.cloned.1.call-update
  254.0 38.6 %all-reduce.2.cloned.1.call-done = f32[512,500]{0,1:T(8,128)} async-done(((f32[512,500]{0,1:T(8,128)}), f32[512,500]{0,1:T(8,128)}) %all-reduce.2.cloned.1.call-update) | async-done | bytes 1024016 | tf_op jit(solution)/shard_map/psum | solution.py:51
  292.6 2.4 add.49
  (17 shorter events, 0.0 us)
Async XLA Ops:
  7.2 1.6 copy-start
  7.2 24.9 %all-gather.3.cloned.1.call-start = ((), (), s32[]{:S(2)}) async-start(), calls=%async_computation.1 | async-start | bytes 3145728 | tf_op jit(solution)/shard_map/all_gather | solution.py:23
  8.8 23.3 %copy-start.2 = (f32[512,500]{0,1:T(8,128)S(1)}, f32[512,500]{0,1:T(8,128)}, u32[]{:S(2)}) copy-start(f32[512,500]{0,1:T(8,128)} %param.12) | copy-start | bytes 3072004
  8.8 23.3 %copy-start.7 = (s32[512]{0:T(512)S(1)}, s32[512]{0:T(512)}, u32[]{:S(2)}) copy-start(s32[512]{0:T(512)} %param.11) | copy-start | bytes 6148
  18.6 95.3 %reduce-scatter.2.cloned.1.call-start = ((), (), s32[]{:S(2)}) async-start(), calls=%async_computation.2 | async-start | bytes 5160960 | tf_op jit(solution)/shard_map/reduce_scatter | solution.py:26
  36.9 212.7 %all-gather.5.cloned.1.call-start = ((), (), s32[]{:S(2)}) async-start(), calls=%async_computation.3 | async-start | bytes 2580480 | tf_op jit(solution)/shard_map/all_gather | solution.py:48
  114.0 26.5 %collective-permute-start = (f32[512,500]{0,1:T(8,128)}, f32[512,500]{0,1:T(8,128)S(1)}, u32[]{:S(2)}, u32[]{:S(2)}) collective-permute-start(f32[512,500]{0,1:T(8,128)} %reduce-scatter.2.cloned.1.call-done), channel_id=1, source_target_pairs={{0,4},{4,8},{8,12},{12,0},{1,5},{5,9},{9,13},{13,1},{2,6},{6,10},{... | collective-permute-start | bytes 3072008 | tf_op jit(solution)/shard_map/ppermute | solution.py:38
  140.5 1.0 copy-start.4
  141.4 25.5 %collective-permute-start.1 = (f32[512,500]{0,1:T(8,128)S(1)}, f32[512,500]{0,1:T(8,128)}, u32[]{:S(2)}, u32[]{:S(2)}) collective-permute-start(f32[512,500]{0,1:T(8,128)S(1)} %collective-permute-done), channel_id=1, source_target_pairs={{0,4},{4,8},{8,12},{12,0},{1,5},{5,9},{9,13},{13,1},{2,6},{6,10},{... | collective-permute-start | bytes 3072008 | tf_op jit(solution)/shard_map/ppermute | solution.py:38
  167.0 24.8 %collective-permute-start.2 = (f32[512,500]{0,1:T(8,128)}, f32[512,500]{0,1:T(8,128)}, u32[]{:S(2)}, u32[]{:S(2)}) collective-permute-start(f32[512,500]{0,1:T(8,128)} %collective-permute-done.1), channel_id=1, source_target_pairs={{0,4},{4,8},{8,12},{12,0},{1,5},{5,9},{9,13},{13,1},{2,6},{6,10},{... | collective-permute-start | bytes 3072008 | tf_op jit(solution)/shard_map/ppermute | solution.py:38
  167.0 27.4 %copy-start.5 = (f32[512,500]{0,1:T(8,128)S(1)}, f32[512,500]{0,1:T(8,128)}, u32[]{:S(2)}) copy-start(f32[512,500]{0,1:T(8,128)} %copy-done.4) | copy-start | bytes 3072004
  167.0 27.5 %copy-start.3 = (f32[512,500]{0,1:T(8,128)S(1)}, f32[512,500]{0,1:T(8,128)}, u32[]{:S(2)}) copy-start(f32[512,500]{0,1:T(8,128)} %reduce-scatter.2.cloned.1.call-done) | copy-start | bytes 3072004
  194.6 3.4 %copy-start.1 = (f32[1,512,2048]{2,1,0:T(8,128)S(1)}, f32[1,512,2048]{2,1,0:T(8,128)}, u32[]{:S(2)}) copy-start(f32[1,512,2048]{2,1,0:T(8,128)} %param.10) | copy-start | bytes 12582916
  194.6 3.4 %copy-start.6 = (f32[512,500]{0,1:T(8,128)S(1)}, f32[512,500]{0,1:T(8,128)}, u32[]{:S(2)}) copy-start(f32[512,500]{0,1:T(8,128)} %param.13) | copy-start | bytes 3072004
  206.0 86.6 %all-reduce.2.cloned.1.call-start = ((), (), s32[]{:S(2)}) async-start(), calls=%async_computation.4 | async-start | bytes 2064384 | tf_op jit(solution)/shard_map/psum | solution.py:51
Sparse Core Ops, SparseCore 0:
  18.8 13.2 all-gather.2
  37.0 76.8 reduce-scatter.1
  206.1 43.4 all-gather.4
  254.2 38.3 all-reduce.1
